TPU v7x, 32 devices: a whole 2x2x4 slice. The times are simulated.
32 devices in a mesh: stn: 8 (over z, core), chan: 4 (over y, x).
Axes of the slice: x: 2, y: 2, z: 4, core: 2. Of those that a mesh axis runs over, the one named last changes fastest.
Arguments:
- voltages: bfloat16 [64, 32, 2, 1024], P('stn', 'chan'), may hold values from -6 to 6
- filter_taps: float32 [16, 1024], replicated, may hold values from -1.5 to 1.5
Outputs:
- visibilities: bfloat16 [1024, 2, 64, 64], P('chan', None, 'stn')
All inputs are finite; a program needn't handle non-finite values.
Results may differ from a plain program's by a relative error of at most 0.0069.
Values may be sent and summed in bfloat16 or wider, within the bound.
A program may use at most 64 MiB of HBM per device.

v0:
```python
import math
import jax
import jax.numpy as jnp
from jax import lax
from jax.sharding import PartitionSpec as P


def from_behind(array, axis, by):
    devices = lax.axis_size(axis)
    pairs = [(i, i + by) for i in range(devices) if 0 <= i + by < devices]
    return lax.ppermute(array, axis, pairs)


def passed_along(value, axis, steps):
    count = lax.axis_size(axis)
    pairs = [(source, (source + steps) % count) for source in range(count)]
    return lax.ppermute(value, axis, pairs)


def fourier_matrix(points):
    sample_index = jnp.arange(points, dtype=jnp.int32)
    phase = sample_index[:, None] * sample_index[None, :] % points
    angle = phase.astype(jnp.float32) * (2.0 * math.pi / points)
    norm_factor = 1.0 / math.sqrt(points)
    cosine = (jnp.cos(angle) * norm_factor).astype(jnp.bfloat16)
    sine_part = (-jnp.sin(angle) * norm_factor).astype(jnp.bfloat16)
    upper_rows = jnp.stack([cosine, sine_part], axis=2)
    lower_rows = jnp.stack([-sine_part, cosine], axis=2)
    return jnp.concatenate([upper_rows, lower_rows], axis=0).reshape(2 * points, 2 * points)


def history_frames(voltages, history_len):
    frames_here = voltages.shape[1]
    shift_count = (history_len - 1) // frames_here + 1
    earlier = []
    for distance in range(1, shift_count + 1):
        keep_count = min(frames_here, history_len - (distance - 1) * frames_here)
        received_frames = from_behind(voltages[:, frames_here - keep_count :], "chan", distance)
        earlier = [received_frames] + earlier
    return jnp.concatenate(earlier + [voltages], axis=1)


def correlate(local_block, swapped, other_block, factor):
    real_part = jnp.einsum(
        "kcas,kcbs->kab", local_block, other_block, preferred_element_type=jnp.float32
    )
    imag_part = jnp.einsum(
        "kcas,kcbs->kab", swapped, other_block, preferred_element_type=jnp.float32
    )
    return jnp.stack([real_part, imag_part], axis=1) * factor


def mirrored(product):
    return jnp.stack(
        [jnp.swapaxes(product[:, 0], 1, 2), -jnp.swapaxes(product[:, 1], 1, 2)], axis=1
    )


def place_block(buffer, product, chan_start, slot_index):
    columns = product.shape[3]
    anchor = jnp.int32(0)
    return lax.dynamic_update_slice(
        buffer, product, (jnp.int32(chan_start), anchor, anchor, slot_index * columns)
    )


def per_device(voltages, filter_taps):
    inputs_here, frames_here, parts, points = voltages.shape
    tap_count = filter_taps.shape[0]
    extended = history_frames(voltages, tap_count - 1)
    filtered = jnp.zeros(voltages.shape, jnp.float32)
    for tap_index in range(tap_count):
        offset = tap_count - 1 - tap_index
        filtered = filtered + filter_taps[tap_index][None, None, None, :] * extended[
            :, offset : offset + frames_here
        ].astype(jnp.float32)
    filtered = filtered.astype(jnp.bfloat16).reshape(inputs_here, frames_here, parts * points)
    matrix = fourier_matrix(points)
    spectra = jnp.einsum("isr,rq->qis", filtered, matrix, preferred_element_type=jnp.float32)
    spectra = spectra.reshape(points, parts, inputs_here, frames_here).astype(jnp.bfloat16)
    local_block = lax.all_to_all(spectra, "chan", split_axis=0, concat_axis=3, tiled=True)
    cycle_size = lax.axis_size("stn")
    position = lax.axis_index("stn")
    halfway = cycle_size // 2
    channels = local_block.shape[0]
    factor = 1.0 / local_block.shape[3]
    swapped = jnp.stack([local_block[:, 1], -local_block[:, 0]], axis=1)
    row_sums = jnp.zeros((channels, parts, inputs_here, cycle_size * inputs_here), jnp.float32)
    row_sums = place_block(
        row_sums, correlate(local_block, swapped, local_block, factor), 0, position
    )
    mirror = jnp.zeros(row_sums.shape, jnp.bfloat16)

    def cycle_turn(step_index, carry):
        moving_block, row_sums, mirror = carry
        moving_block = passed_along(moving_block, "stn", -1)
        slot_index = (position + step_index) % cycle_size
        is_kept = jnp.logical_or(step_index < halfway, position < halfway)
        product = jnp.where(is_kept, correlate(local_block, swapped, moving_block, factor), 0.0)
        row_sums = place_block(row_sums, product, 0, slot_index)
        outgoing = mirrored(product).astype(jnp.bfloat16)
        mirror = place_block(mirror, outgoing, 0, slot_index)
        return (moving_block, row_sums, mirror)

    moving_block, row_sums, mirror = lax.fori_loop(
        1, halfway + 1, cycle_turn, (local_block, row_sums, mirror)
    )
    returned = lax.all_to_all(mirror, "stn", split_axis=3, concat_axis=3, tiled=True)
    row_sums = row_sums + returned.astype(jnp.float32)
    return row_sums.astype(jnp.bfloat16)


def solution(mesh):
    placed = (P("stn", "chan", None, None), P())
    return jax.shard_map(
        per_device,
        mesh=mesh,
        in_specs=placed,
        out_specs=P("chan", None, "stn", None),
        check_vma=False,
    )
```

profile of v0, /device:TPU:0, one launch (start us, length us, event | category | flops | bytes accessed | tf_op | source)
XLA Modules:
  0.0 217.8 jit_solution(14949994201829251121)
XLA Ops:
  0.0 4.8 %collective-permute-start.1 = (bf16[8,8,2,1024]{3,2,1,0:T(2,128)(2,1)}, bf16[8,8,2,1024]{3,2,1,0:T(2,128)(2,1)S(1)}, u32[]{:S(2)}, u32[]{:S(2)}) collective-permute-start(bf16[8,8,2,1024]{3,2,1,0:T(2,128)(2,1)} %param.4), channel_id=1, source_target_pairs={{0,1},{1,2},{2,3},{4,5},{5,6},{6,7},{8,9},{9,10},{10,11},{12,13},{... | collective-permute-start | bytes 786440 | tf_op jit(solution)/shard_map/ppermute | solution.py:11
  6.0 3.4 %collective-permute-start.2 = (bf16[8,7,2,1024]{3,2,1,0:T(2,128)(2,1)S(1)}, bf16[8,7,2,1024]{3,2,1,0:T(2,128)(2,1)S(1)}, u32[]{:S(2)}, u32[]{:S(2)}) collective-permute-start(bf16[8,7,2,1024]{3,2,1,0:T(2,128)(2,1)S(1)} %slice.151), channel_id=1, source_target_pairs={{0,2},{1,3},{4,6},{5,7},{8,10},{9,11},{12,14},{13,15},{16,18},{17,... | collective-permute-start | bytes 688136 | tf_op jit(solution)/shard_map/ppermute | solution.py:11
  9.4 17.1 %multiply_convert_fusion = (bf16[1024,1024,1]{1,0,2:T(8,128)(2,1)S(1)}, bf16[1024,1024,1]{1,0,2:T(8,128)(2,1)S(1)}) fusion(), kind=kLoop, calls=%fused_computation.21 | loop fusion | flops 19922944 | bytes 4194304 | tf_op jit(solution)/shard_map/convert_element_type | solution.py:26
  26.6 15.8 %fusion.16 = bf16[1024,1024,1]{1,0,2:T(8,128)(2,1)S(1)} fusion(), kind=kLoop, calls=%fused_computation.31 | loop fusion | flops 20971520 | bytes 2097152 | tf_op jit(solution)/shard_map/neg | solution.py:28
  42.4 4.0 %maximum_maximum_fusion = bf16[2048,1024,2]{1,0,2:T(8,128)(2,1)} fusion(bf16[1024,1024,1]{1,0,2:T(8,128)(2,1)S(1)} %get-tuple-element.262, bf16[1024,1024,1]{1,0,2:T(8,128)(2,1)S(1)} %fusion.16, bf16[1024,1024,1]{1,0,2:T(8,128)(2,1)S(1)} %get-tuple-element.261), kind=kLoop, calls=%fused_computation.12 | loop fusion | flops 33554432 | bytes 14680064 | tf_op jit(solution)/shard_map/concatenate | solution.py:29
  46.4 21.5 %copy.62 = bf16[2048,1024,2]{0,2,1:T(2,128)(2,1)} copy(bf16[2048,1024,2]{1,0,2:T(8,128)(2,1)} %maximum_maximum_fusion) | data formatting | bytes 16777216 | tf_op jit(solution)/shard_map/concatenate | solution.py:29
  67.9 13.1 %reshape.119 = bf16[2048,2048]{0,1:T(8,128)(2,1)} reshape(bf16[2048,1024,2]{0,2,1:T(2,128)(2,1)} %copy.62) | data formatting | bytes 16777216 | tf_op jit(solution)/shard_map/reshape | solution.py:29
  81.0 14.2 %dot_general.34 = bf16[1024,2,2048]{2,1,0:T(2,128)(2,1)} reshape(bf16[2048,2048]{1,0:T(8,128)(2,1)} %bitcast.78) | data formatting | bytes 16777216 | tf_op jit(solution)/shard_map/isr,rq->qis/dot_general | solution.py:79
  96.0 3.8 %add_convert_fusion = bf16[8,8,2,1024]{3,2,1,0:T(2,128)(2,1)S(1)} fusion(bf16[8,8,2,1024]{3,2,1,0:T(2,128)(2,1)S(1)} %collective-permute-done.1, bf16[8,8,2,1024]{3,2,1,0:T(2,128)(2,1)S(1)} %copy-done.1, bf16[8,15,2,1024]{3,2,1,0:T(2,128)(2,1)S(1)} %get-tuple-element.244, bf16[8,16,2,1024]{3,2,1,0:T(2,128)(2,1)S(1)} %constant_dynamic-update-slice_fusion.1, ...), kind=kLoop, calls=%fused_computation.32 | loop fusion | flops 6291456 | bytes 4521984 | tf_op jit(solution)/shard_map/convert_element_type | solution.py:77
  100.0 8.2 %fusion.12 = bf16[1024,2,8,8]{0,3,2,1:T(8,128)(2,1)S(1)} fusion(bf16[8,8,2048,1]{2,1,0,3:T(8,128)(2,1)S(1)} %reshape.124, bf16[1024,2,2048,1]{2,1,0,3:T(2,128)(2,1)} %bitcast.80), kind=kOutput, calls=%fused_computation.28 | convolution fusion | flops 537001984 | bytes 8912896 | tf_op jit(solution)/shard_map/isr,rq->qis/dot_general | solution.py:79
  108.3 4.7 %copy.64 = bf16[1024,2,8,8]{3,2,1,0:T(8,128)(2,1)} copy(bf16[1024,2,8,8]{0,3,2,1:T(8,128)(2,1)S(1)} %fusion.12) | data formatting | bytes 524288 | tf_op jit(solution)/shard_map/convert_element_type | solution.py:80
  113.0 6.4 %reshape.128 = bf16[4,2,16384]{2,1,0:T(2,128)(2,1)} reshape(bf16[1024,2,8,8]{3,2,1,0:T(8,128)(2,1)} %copy.64) | data formatting | bytes 524288
  119.4 3.4 %all-to-all-start = ((bf16[4,2,16384]{2,1,0:T(2,128)(2,1)}), bf16[4,2,16384]{2,1,0:T(2,128)(2,1)S(1)}, u32[]{:S(2)}, u32[]{:S(2)}) async-start(bf16[4,2,16384]{2,1,0:T(2,128)(2,1)} %reshape.128), calls=%async_computation | async-start | bytes 524288 | tf_op jit(solution)/shard_map/all_to_all | solution.py:81
  122.8 5.3 %all-to-all-done = bf16[4,2,16384]{2,1,0:T(2,128)(2,1)S(1)} async-done(((bf16[4,2,16384]{2,1,0:T(2,128)(2,1)}), bf16[4,2,16384]{2,1,0:T(2,128)(2,1)S(1)}, u32[]{:S(2)}, u32[]{:S(2)}) %all-to-all-start) | async-done | bytes 262176 | tf_op jit(solution)/shard_map/all_to_all | solution.py:81
  128.1 5.9 %reshape.129 = bf16[1024,2,8,8]{3,2,1,0:T(8,128)(2,1)} reshape(bf16[4,2,16384]{2,1,0:T(2,128)(2,1)S(1)} %all-to-all-done) | data formatting | bytes 524288
  134.1 4.7 %copy.85 = bf16[4,256,2,8,8]{1,0,4,3,2:T(4,128)(2,1)S(1)} copy(bf16[4,256,2,8,8]{4,3,2,1,0:T(8,128)(2,1)} %bitcast.79) | data formatting | bytes 524288 | tf_op jit(solution)/shard_map/all_to_all | solution.py:81
  139.8 1.9 copy.69
  142.1 1.6 convolution_bitcast_fusion.2
  145.8 48.9 %while.19 = (s32[]{:T(128)}, bf16[256,2,8,32]{0,3,2,1:T(8,128)(2,1)S(1)}, f32[256,2,8,64]{0,3,2,1:T(8,128)}, bf16[256,2,8,64]{0,2,1,3:T(8,128)(2,1)}, pred[]{:T(...) while((s32[]{:T(128)}, ...), condition=%wide.region_1.2_spmd, body=%wide.region_0.1_spmd.sunk | while | flops 4358164 | bytes 4489577 | solution.py:105
  147.1 3.9 %collective-permute-done = bf16[256,2,8,32]{0,3,2,1:T(8,128)(2,1)S(1)} collective-permute-done((bf16[256,2,8,32]{0,3,2,1:T(8,128)(2,1)S(1)}, bf16[256,2,8,32]{0,3,2,1:T(8,128)(2,1)S(1)}, u32[]{:S(2)}, u32[]{:S(2)}) %collective-permute-start) | collective-permute-done | bytes 262176 | tf_op jit(solution)/shard_map/while/body/eval_jaxpr/ppermute | solution.py:17
  152.0 1.6 convolution_bitcast_fusion.6
  156.2 3.8 %collective-permute-start = (bf16[256,2,8,32]{0,3,2,1:T(8,128)(2,1)S(1)}, bf16[256,2,8,32]{0,3,2,1:T(8,128)(2,1)S(1)}, u32[]{:S(2)}, u32[]{:S(2)}) collective-permute-start(bf16[256,2,8,32]{0,3,2,1:T(8,128)(2,1)S(1)} %get-tuple-element.331), channel_id=1, source_target_pairs={{0,28},{4,0},{8,4},{12,8},{16,12},{20,16},{24,20},{28,24},{1,29},{... | collective-permute-start | bytes 786440 | tf_op jit(solution)/shard_map/while/body/eval_jaxpr/ppermute | solution.py:17
  160.0 3.9 %collective-permute-done = bf16[256,2,8,32]{0,3,2,1:T(8,128)(2,1)S(1)} collective-permute-done((bf16[256,2,8,32]{0,3,2,1:T(8,128)(2,1)S(1)}, bf16[256,2,8,32]{0,3,2,1:T(8,128)(2,1)S(1)}, u32[]{:S(2)}, u32[]{:S(2)}) %collective-permute-start) | collective-permute-done | bytes 262176 | tf_op jit(solution)/shard_map/while/body/eval_jaxpr/ppermute | solution.py:17
  164.8 1.6 convolution_bitcast_fusion.6
  169.0 3.8 %collective-permute-start = (bf16[256,2,8,32]{0,3,2,1:T(8,128)(2,1)S(1)}, bf16[256,2,8,32]{0,3,2,1:T(8,128)(2,1)S(1)}, u32[]{:S(2)}, u32[]{:S(2)}) collective-permute-start(bf16[256,2,8,32]{0,3,2,1:T(8,128)(2,1)S(1)} %get-tuple-element.331), channel_id=1, source_target_pairs={{0,28},{4,0},{8,4},{12,8},{16,12},{20,16},{24,20},{28,24},{1,29},{... | collective-permute-start | bytes 786440 | tf_op jit(solution)/shard_map/while/body/eval_jaxpr/ppermute | solution.py:17
  172.8 3.9 %collective-permute-done = bf16[256,2,8,32]{0,3,2,1:T(8,128)(2,1)S(1)} collective-permute-done((bf16[256,2,8,32]{0,3,2,1:T(8,128)(2,1)S(1)}, bf16[256,2,8,32]{0,3,2,1:T(8,128)(2,1)S(1)}, u32[]{:S(2)}, u32[]{:S(2)}) %collective-permute-start) | collective-permute-done | bytes 262176 | tf_op jit(solution)/shard_map/while/body/eval_jaxpr/ppermute | solution.py:17
  177.7 1.6 convolution_bitcast_fusion.6
  181.9 3.7 %collective-permute-start = (bf16[256,2,8,32]{0,3,2,1:T(8,128)(2,1)S(1)}, bf16[256,2,8,32]{0,3,2,1:T(8,128)(2,1)S(1)}, u32[]{:S(2)}, u32[]{:S(2)}) collective-permute-start(bf16[256,2,8,32]{0,3,2,1:T(8,128)(2,1)S(1)} %get-tuple-element.331), channel_id=1, source_target_pairs={{0,28},{4,0},{8,4},{12,8},{16,12},{20,16},{24,20},{28,24},{1,29},{... | collective-permute-start | bytes 786440 | tf_op jit(solution)/shard_map/while/body/eval_jaxpr/ppermute | solution.py:17
  185.6 3.9 %collective-permute-done = bf16[256,2,8,32]{0,3,2,1:T(8,128)(2,1)S(1)} collective-permute-done((bf16[256,2,8,32]{0,3,2,1:T(8,128)(2,1)S(1)}, bf16[256,2,8,32]{0,3,2,1:T(8,128)(2,1)S(1)}, u32[]{:S(2)}, u32[]{:S(2)}) %collective-permute-start) | collective-permute-done | bytes 262176 | tf_op jit(solution)/shard_map/while/body/eval_jaxpr/ppermute | solution.py:17
  190.5 1.6 convolution_bitcast_fusion.6
  194.7 20.3 %all_to_all.23 = bf16[256,2,8,64]{0,2,1,3:T(8,128)(2,1)S(1)} all-to-all(bf16[256,2,8,64]{0,2,1,3:T(8,128)(2,1)} %get-tuple-element.190), channel_id=1, replica_groups=mesh['stn'=8,'chan'=4] {'stn'}, dimensions={3} | all-to-all | bytes 1048576 | tf_op jit(solution)/shard_map/all_to_all | solution.py:108
  215.1 1.8 fusion.15
  (74 shorter events, 21.9 us)
Async XLA Ops:
  0.0 95.4 %collective-permute-start.1 = (bf16[8,8,2,1024]{3,2,1,0:T(2,128)(2,1)}, bf16[8,8,2,1024]{3,2,1,0:T(2,128)(2,1)S(1)}, u32[]{:S(2)}, u32[]{:S(2)}) collective-permute-start(bf16[8,8,2,1024]{3,2,1,0:T(2,128)(2,1)} %param.4), channel_id=1, source_target_pairs={{0,1},{1,2},{2,3},{4,5},{5,6},{6,7},{8,9},{9,10},{10,11},{12,13},{... | collective-permute-start | bytes 786440 | tf_op jit(solution)/shard_map/ppermute | solution.py:11
  6.0 89.2 %collective-permute-start.2 = (bf16[8,7,2,1024]{3,2,1,0:T(2,128)(2,1)S(1)}, bf16[8,7,2,1024]{3,2,1,0:T(2,128)(2,1)S(1)}, u32[]{:S(2)}, u32[]{:S(2)}) collective-permute-start(bf16[8,7,2,1024]{3,2,1,0:T(2,128)(2,1)S(1)} %slice.151), channel_id=1, source_target_pairs={{0,2},{1,3},{4,6},{5,7},{8,10},{9,11},{12,14},{13,15},{16,18},{17,... | collective-permute-start | bytes 688136 | tf_op jit(solution)/shard_map/ppermute | solution.py:11
  81.0 14.2 %copy-start.2 = (f32[16,1024]{1,0:T(8,128)S(1)}, f32[16,1024]{1,0:T(8,128)}, u32[]{:S(2)}) copy-start(f32[16,1024]{1,0:T(8,128)} %param.5) | copy-start | bytes 196612
  81.0 14.8 %copy-start.1 = (bf16[8,8,2,1024]{3,2,1,0:T(2,128)(2,1)S(1)}, bf16[8,8,2,1024]{3,2,1,0:T(2,128)(2,1)}, u32[]{:S(2)}) copy-start(bf16[8,8,2,1024]{3,2,1,0:T(2,128)(2,1)} %param.4) | copy-start | bytes 786436
  119.4 8.8 %all-to-all-start = ((bf16[4,2,16384]{2,1,0:T(2,128)(2,1)}), bf16[4,2,16384]{2,1,0:T(2,128)(2,1)S(1)}, u32[]{:S(2)}, u32[]{:S(2)}) async-start(bf16[4,2,16384]{2,1,0:T(2,128)(2,1)} %reshape.128), calls=%async_computation | async-start | bytes 524288 | tf_op jit(solution)/shard_map/all_to_all | solution.py:81
  144.6 1.2 copy-start
  145.8 5.2 %collective-permute-start = (bf16[256,2,8,32]{0,3,2,1:T(8,128)(2,1)S(1)}, bf16[256,2,8,32]{0,3,2,1:T(8,128)(2,1)S(1)}, u32[]{:S(2)}, u32[]{:S(2)}) collective-permute-start(bf16[256,2,8,32]{0,3,2,1:T(8,128)(2,1)S(1)} %get-tuple-element.331), channel_id=1, source_target_pairs={{0,28},{4,0},{8,4},{12,8},{16,12},{20,16},{24,20},{28,24},{1,29},{... | collective-permute-start | bytes 786440 | tf_op jit(solution)/shard_map/while/body/eval_jaxpr/ppermute | solution.py:17
  156.2 7.7 %collective-permute-start = (bf16[256,2,8,32]{0,3,2,1:T(8,128)(2,1)S(1)}, bf16[256,2,8,32]{0,3,2,1:T(8,128)(2,1)S(1)}, u32[]{:S(2)}, u32[]{:S(2)}) collective-permute-start(bf16[256,2,8,32]{0,3,2,1:T(8,128)(2,1)S(1)} %get-tuple-element.331), channel_id=1, source_target_pairs={{0,28},{4,0},{8,4},{12,8},{16,12},{20,16},{24,20},{28,24},{1,29},{... | collective-permute-start | bytes 786440 | tf_op jit(solution)/shard_map/while/body/eval_jaxpr/ppermute | solution.py:17
  169.0 7.7 %collective-permute-start = (bf16[256,2,8,32]{0,3,2,1:T(8,128)(2,1)S(1)}, bf16[256,2,8,32]{0,3,2,1:T(8,128)(2,1)S(1)}, u32[]{:S(2)}, u32[]{:S(2)}) collective-permute-start(bf16[256,2,8,32]{0,3,2,1:T(8,128)(2,1)S(1)} %get-tuple-element.331), channel_id=1, source_target_pairs={{0,28},{4,0},{8,4},{12,8},{16,12},{20,16},{24,20},{28,24},{1,29},{... | collective-permute-start | bytes 786440 | tf_op jit(solution)/shard_map/while/body/eval_jaxpr/ppermute | solution.py:17
  181.9 7.6 %collective-permute-start = (bf16[256,2,8,32]{0,3,2,1:T(8,128)(2,1)S(1)}, bf16[256,2,8,32]{0,3,2,1:T(8,128)(2,1)S(1)}, u32[]{:S(2)}, u32[]{:S(2)}) collective-permute-start(bf16[256,2,8,32]{0,3,2,1:T(8,128)(2,1)S(1)} %get-tuple-element.331), channel_id=1, source_target_pairs={{0,28},{4,0},{8,4},{12,8},{16,12},{20,16},{24,20},{28,24},{1,29},{... | collective-permute-start | bytes 786440 | tf_op jit(solution)/shard_map/while/body/eval_jaxpr/ppermute | solution.py:17
where the time goes:
time: 220 us; the launch traced here: 218 us
  local copies, waits for them, and re-layouts  87.8 us (40%)
  other arithmetic  45.6 us (21%)
  starting transfers between devices  24.3 us (11%)
  waiting for transfers between devices  20.9 us (10%)
  blocking collectives  20.3 us (9%)
  matrix products  18.5 us (8%)
    concatenate x1, local copies, waits for them, and re-layouts, fourier_matrix(): jnp.concatenate([upper_rows, lower_rows], axis=0)  21.5 us
    all_to_all x1, blocking collectives, per_device(): lax.all_to_all(mirror, 'stn', split_axis=3, concat_axis=3, tiled=True)  20.3 us
    convert_element_type x1, other arithmetic, fourier_matrix(): sine_part = (-jnp.sin(angle) * norm_factor).astype(jnp.bfloat16)  17.1 us
    neg x1, other arithmetic, fourier_matrix(): lower_rows = jnp.stack([-sine_part, cosine], axis=2)  15.8 us
    ppermute x4, waiting for transfers between devices, passed_along(): return lax.ppermute(value, axis, pairs)  15.6 us
    dot_general x1, local copies, waits for them, and re-layouts, per_device(): jnp.einsum('isr,rq->qis', filtered, matrix, preferred_element_type=jnp.fl...  14.2 us
    unnamed x10, local copies, waits for them, and re-layouts  13.2 us
    reshape x1, local copies, waits for them, and re-layouts, fourier_matrix(): jnp.concatenate([upper_rows, lower_rows], axis=0)  13.1 us
  transfers between devices with their start and end apart: 7, of which 5 were waited for; matrix products, arithmetic and copies ran while one was open for 40% of the time, Pallas kernels for 0%

commit v1 on v0

--- a/solution.py
+++ b/solution.py
@@ -3,6 +3,29 @@
 import jax.numpy as jnp
 from jax import lax
 from jax.sharding import PartitionSpec as P
+
+
+def cut_along(array, dim, devices):
+    dims = array.shape
+    blocks = array.reshape(*dims[:dim], devices, dims[dim] // devices, *dims[dim + 1 :])
+    return jnp.moveaxis(blocks, dim, 0)
+
+
+def laid_out(tiles, dim):
+    shape = list(tiles.shape[1:])
+    shape[dim] *= tiles.shape[0]
+    return jnp.moveaxis(tiles, 0, dim).reshape(shape)
+
+
+def rotated_exchange(array, axis, split_dim, concat_dim):
+    length, mine = (lax.axis_size(axis), lax.axis_index(axis))
+    blocks = cut_along(array, split_dim, length)
+    outs = [blocks[mine]]
+    for hop in range(1, length):
+        sent = blocks[(mine + hop) % length]
+        outs.append(lax.ppermute(sent, axis, [(i, (i + hop) % length) for i in range(length)]))
+    blocks = jnp.stack(outs)[(mine - jnp.arange(length)) % length]
+    return laid_out(blocks, concat_dim)
 
 
 def from_behind(array, axis, by):
@@ -105,7 +128,7 @@
     moving_block, row_sums, mirror = lax.fori_loop(
         1, halfway + 1, cycle_turn, (local_block, row_sums, mirror)
     )
-    returned = lax.all_to_all(mirror, "stn", split_axis=3, concat_axis=3, tiled=True)
+    returned = rotated_exchange(mirror, "stn", 3, 3)
     row_sums = row_sums + returned.astype(jnp.float32)
     return row_sums.astype(jnp.bfloat16)
 

time: 220 us -> 218 us (level)
  blocking collectives: 20.3 us -> 0 us
  starting transfers between devices: 24.3 us -> 32.5 us
  other arithmetic: 45.6 us -> 51.3 us
  waiting for transfers between devices: 20.9 us -> 26.1 us
    all_to_all x1 -> x0, blocking collectives: 20.3 us -> none  [per_device(): lax.all_to_all(mirror, 'stn', split_axis=3, concat_axis=3, tiled=True)]
    ppermute x0 -> x7, starting transfers between devices: none -> 8.29 us  [rotated_exchange(): lax.ppermute(sent, axis, [(i, (i + hop) % length) for i in range(length)])]
    ppermute x0 -> x7, waiting for transfers between devices: none -> 5.2 us  [rotated_exchange(): lax.ppermute(sent, axis, [(i, (i + hop) % length) for i in range(length)])]
    dynamic_update_slice x5 -> x9, other arithmetic: 2.84 us -> 5.51 us  [place_block(): lax.dynamic_update_slice(buffer, product, (jnp.int32(chan_start), anchor,...]
    dynamic_update_slice x4 -> x0, local copies, waits for them, and re-layouts: 2.6 us -> none  [place_block(): lax.dynamic_update_slice(buffer, product, (jnp.int32(chan_start), anchor,...]
    concatenate x1, other arithmetic: 4.04 us -> 6.57 us  [fourier_matrix(): jnp.concatenate([upper_rows, lower_rows], axis=0)]
    unnamed x10 -> x19, local copies, waits for them, and re-layouts: 13.2 us -> 14.6 us
  transfers between devices with their start and end apart: 7 -> 14, of which waited for: 5 -> 8; matrix products, arithmetic and copies ran while one was open for 40% -> 43% of each run, Pallas kernels for 0% -> 0%
where the time goes in v1:
time: 218 us; the launch traced here: 216 us
  local copies, waits for them, and re-layouts  87.5 us (40%)
  other arithmetic  51.3 us (24%)
  starting transfers between devices  32.5 us (15%)
  waiting for transfers between devices  26.1 us (12%)
  matrix products  18.5 us (8%)
    concatenate x1, local copies, waits for them, and re-layouts, fourier_matrix(): jnp.concatenate([upper_rows, lower_rows], axis=0)  21.5 us
    convert_element_type x1, other arithmetic, fourier_matrix(): sine_part = (-jnp.sin(angle) * norm_factor).astype(jnp.bfloat16)  17.9 us
    neg x1, other arithmetic, fourier_matrix(): lower_rows = jnp.stack([-sine_part, cosine], axis=2)  16.5 us
    ppermute x4, waiting for transfers between devices, passed_along(): return lax.ppermute(value, axis, pairs)  15.6 us
    unnamed x19, local copies, waits for them, and re-layouts  14.6 us
    dot_general x1, local copies, waits for them, and re-layouts, per_device(): jnp.einsum('isr,rq->qis', filtered, matrix, preferred_element_type=jnp.fl...  14.2 us
    reshape x1, local copies, waits for them, and re-layouts, fourier_matrix(): jnp.concatenate([upper_rows, lower_rows], axis=0)  13.1 us
    ppermute x4, starting transfers between devices, passed_along(): return lax.ppermute(value, axis, pairs)  12.6 us
  transfers between devices with their start and end apart: 14, of which 8 were waited for; matrix products, arithmetic and copies ran while one was open for 43% of the time, Pallas kernels for 0%

profile of v1, /device:TPU:0, one launch (start us, length us, event | category | flops | bytes accessed | tf_op | source)
XLA Modules:
  0.0 216.4 jit_solution(13094917617574337028)
XLA Ops:
  0.0 4.8 %collective-permute-start.1 = (bf16[8,8,2,1024]{3,2,1,0:T(2,128)(2,1)}, bf16[8,8,2,1024]{3,2,1,0:T(2,128)(2,1)S(1)}, u32[]{:S(2)}, u32[]{:S(2)}) collective-permute-start(bf16[8,8,2,1024]{3,2,1,0:T(2,128)(2,1)} %param.4), channel_id=1, source_target_pairs={{0,1},{1,2},{2,3},{4,5},{5,6},{6,7},{8,9},{9,10},{10,11},{12,13},{... | collective-permute-start | bytes 786440 | tf_op jit(solution)/shard_map/ppermute | solution.py:34
  6.0 3.4 %collective-permute-start.2 = (bf16[8,7,2,1024]{3,2,1,0:T(2,128)(2,1)S(1)}, bf16[8,7,2,1024]{3,2,1,0:T(2,128)(2,1)S(1)}, u32[]{:S(2)}, u32[]{:S(2)}) collective-permute-start(bf16[8,7,2,1024]{3,2,1,0:T(2,128)(2,1)S(1)} %slice.151), channel_id=1, source_target_pairs={{0,2},{1,3},{4,6},{5,7},{8,10},{9,11},{12,14},{13,15},{16,18},{17,... | collective-permute-start | bytes 688136 | tf_op jit(solution)/shard_map/ppermute | solution.py:34
  9.4 17.9 %multiply_convert_fusion = (bf16[1024,1024,1]{1,0,2:T(8,128)(2,1)S(1)}, bf16[1024,1024,1]{1,0,2:T(8,128)(2,1)}) fusion(), kind=kLoop, calls=%fused_computation.21 | loop fusion | flops 19922944 | bytes 4194304 | tf_op jit(solution)/shard_map/convert_element_type | solution.py:49
  27.3 16.5 %fusion.16 = bf16[1024,1024,1]{1,0,2:T(8,128)(2,1)} fusion(), kind=kLoop, calls=%fused_computation.32 | loop fusion | flops 20971520 | bytes 2097152 | tf_op jit(solution)/shard_map/neg | solution.py:51
  43.8 6.6 %maximum_maximum_fusion = bf16[2048,1024,2]{1,0,2:T(8,128)(2,1)} fusion(bf16[1024,1024,1]{1,0,2:T(8,128)(2,1)} %get-tuple-element.277, bf16[1024,1024,1]{1,0,2:T(8,128)(2,1)} %fusion.16, bf16[1024,1024,1]{1,0,2:T(8,128)(2,1)S(1)} %get-tuple-element.276), kind=kLoop, calls=%fused_computation.12 | loop fusion | flops 33554432 | bytes 14680064 | tf_op jit(solution)/shard_map/concatenate | solution.py:52
  50.4 21.5 %copy.98 = bf16[2048,1024,2]{0,2,1:T(2,128)(2,1)} copy(bf16[2048,1024,2]{1,0,2:T(8,128)(2,1)} %maximum_maximum_fusion) | data formatting | bytes 16777216 | tf_op jit(solution)/shard_map/concatenate | solution.py:52
  71.8 13.1 %reshape.189 = bf16[2048,2048]{0,1:T(8,128)(2,1)} reshape(bf16[2048,1024,2]{0,2,1:T(2,128)(2,1)} %copy.98) | data formatting | bytes 16777216 | tf_op jit(solution)/shard_map/reshape | solution.py:52
  85.0 14.2 %dot_general.34 = bf16[1024,2,2048]{2,1,0:T(2,128)(2,1)} reshape(bf16[2048,2048]{1,0:T(8,128)(2,1)} %bitcast.134) | data formatting | bytes 16777216 | tf_op jit(solution)/shard_map/isr,rq->qis/dot_general | solution.py:102
  100.1 3.8 %add_convert_fusion = bf16[8,8,2,1024]{3,2,1,0:T(2,128)(2,1)S(1)} fusion(bf16[8,8,2,1024]{3,2,1,0:T(2,128)(2,1)S(1)} %collective-permute-done.1, bf16[8,8,2,1024]{3,2,1,0:T(2,128)(2,1)S(1)} %copy-done.2, bf16[8,15,2,1024]{3,2,1,0:T(2,128)(2,1)S(1)} %get-tuple-element.259, bf16[8,16,2,1024]{3,2,1,0:T(2,128)(2,1)S(1)} %constant_dynamic-update-slice_fusion.1, ...), kind=kLoop, calls=%fused_computation.33 | loop fusion | flops 6291456 | bytes 4521984 | tf_op jit(solution)/shard_map/convert_element_type | solution.py:100
  104.1 8.2 %fusion.12 = bf16[1024,2,8,8]{0,3,2,1:T(8,128)(2,1)S(1)} fusion(bf16[8,8,2048,1]{2,1,0,3:T(8,128)(2,1)S(1)} %reshape.204, bf16[1024,2,2048,1]{2,1,0,3:T(2,128)(2,1)} %bitcast.136), kind=kOutput, calls=%fused_computation.28 | convolution fusion | flops 537001984 | bytes 8912896 | tf_op jit(solution)/shard_map/isr,rq->qis/dot_general | solution.py:102
  112.3 4.7 %copy.100 = bf16[1024,2,8,8]{3,2,1,0:T(8,128)(2,1)} copy(bf16[1024,2,8,8]{0,3,2,1:T(8,128)(2,1)S(1)} %fusion.12) | data formatting | bytes 524288 | tf_op jit(solution)/shard_map/convert_element_type | solution.py:103
  117.0 6.4 %reshape.208 = bf16[4,2,16384]{2,1,0:T(2,128)(2,1)} reshape(bf16[1024,2,8,8]{3,2,1,0:T(8,128)(2,1)} %copy.100) | data formatting | bytes 524288
  123.4 3.4 %all-to-all-start = ((bf16[4,2,16384]{2,1,0:T(2,128)(2,1)}), bf16[4,2,16384]{2,1,0:T(2,128)(2,1)S(1)}, u32[]{:S(2)}, u32[]{:S(2)}) async-start(bf16[4,2,16384]{2,1,0:T(2,128)(2,1)} %reshape.208), calls=%async_computation | async-start | bytes 524288 | tf_op jit(solution)/shard_map/all_to_all | solution.py:104
  126.8 5.3 %all-to-all-done = bf16[4,2,16384]{2,1,0:T(2,128)(2,1)S(1)} async-done(((bf16[4,2,16384]{2,1,0:T(2,128)(2,1)}), bf16[4,2,16384]{2,1,0:T(2,128)(2,1)S(1)}, u32[]{:S(2)}, u32[]{:S(2)}) %all-to-all-start) | async-done | bytes 262176 | tf_op jit(solution)/shard_map/all_to_all | solution.py:104
  132.1 5.9 %reshape.209 = bf16[1024,2,8,8]{3,2,1,0:T(8,128)(2,1)} reshape(bf16[4,2,16384]{2,1,0:T(2,128)(2,1)S(1)} %all-to-all-done) | data formatting | bytes 524288
  138.1 4.7 %copy.127 = bf16[4,256,2,8,8]{1,0,4,3,2:T(4,128)(2,1)S(1)} copy(bf16[4,256,2,8,8]{4,3,2,1,0:T(8,128)(2,1)} %bitcast.135) | data formatting | bytes 524288 | tf_op jit(solution)/shard_map/all_to_all | solution.py:104
  143.8 1.9 copy.105
  146.1 1.6 convolution_bitcast_fusion.2
  149.8 48.9 %while.19 = (s32[]{:T(128)}, bf16[256,2,8,32]{0,3,2,1:T(8,128)(2,1)S(1)}, f32[256,2,8,64]{0,3,2,1:T(8,128)}, bf16[256,2,8,64]{0,3,2,1:T(8,128)(2,1)}, pred[]{:T(...) while((s32[]{:T(128)}, ...), condition=%wide.region_1.2_spmd, body=%wide.region_0.1_spmd.sunk | while | flops 4456468 | bytes 4358505 | solution.py:128
  151.1 3.9 %collective-permute-done = bf16[256,2,8,32]{0,3,2,1:T(8,128)(2,1)S(1)} collective-permute-done((bf16[256,2,8,32]{0,3,2,1:T(8,128)(2,1)S(1)}, bf16[256,2,8,32]{0,3,2,1:T(8,128)(2,1)S(1)}, u32[]{:S(2)}, u32[]{:S(2)}) %collective-permute-start) | collective-permute-done | bytes 262176 | tf_op jit(solution)/shard_map/while/body/eval_jaxpr/ppermute | solution.py:40
  160.2 3.7 %collective-permute-start = (bf16[256,2,8,32]{0,3,2,1:T(8,128)(2,1)S(1)}, bf16[256,2,8,32]{0,3,2,1:T(8,128)(2,1)S(1)}, u32[]{:S(2)}, u32[]{:S(2)}) collective-permute-start(bf16[256,2,8,32]{0,3,2,1:T(8,128)(2,1)S(1)} %get-tuple-element.346), channel_id=1, source_target_pairs={{0,28},{4,0},{8,4},{12,8},{16,12},{20,16},{24,20},{28,24},{1,29},{... | collective-permute-start | bytes 786440 | tf_op jit(solution)/shard_map/while/body/eval_jaxpr/ppermute | solution.py:40
  163.9 3.9 %collective-permute-done = bf16[256,2,8,32]{0,3,2,1:T(8,128)(2,1)S(1)} collective-permute-done((bf16[256,2,8,32]{0,3,2,1:T(8,128)(2,1)S(1)}, bf16[256,2,8,32]{0,3,2,1:T(8,128)(2,1)S(1)}, u32[]{:S(2)}, u32[]{:S(2)}) %collective-permute-start) | collective-permute-done | bytes 262176 | tf_op jit(solution)/shard_map/while/body/eval_jaxpr/ppermute | solution.py:40
  173.0 3.7 %collective-permute-start = (bf16[256,2,8,32]{0,3,2,1:T(8,128)(2,1)S(1)}, bf16[256,2,8,32]{0,3,2,1:T(8,128)(2,1)S(1)}, u32[]{:S(2)}, u32[]{:S(2)}) collective-permute-start(bf16[256,2,8,32]{0,3,2,1:T(8,128)(2,1)S(1)} %get-tuple-element.346), channel_id=1, source_target_pairs={{0,28},{4,0},{8,4},{12,8},{16,12},{20,16},{24,20},{28,24},{1,29},{... | collective-permute-start | bytes 786440 | tf_op jit(solution)/shard_map/while/body/eval_jaxpr/ppermute | solution.py:40
  176.8 3.9 %collective-permute-done = bf16[256,2,8,32]{0,3,2,1:T(8,128)(2,1)S(1)} collective-permute-done((bf16[256,2,8,32]{0,3,2,1:T(8,128)(2,1)S(1)}, bf16[256,2,8,32]{0,3,2,1:T(8,128)(2,1)S(1)}, u32[]{:S(2)}, u32[]{:S(2)}) %collective-permute-start) | collective-permute-done | bytes 262176 | tf_op jit(solution)/shard_map/while/body/eval_jaxpr/ppermute | solution.py:40
  181.6 1.6 convolution_bitcast_fusion.6
  185.8 3.8 %collective-permute-start = (bf16[256,2,8,32]{0,3,2,1:T(8,128)(2,1)S(1)}, bf16[256,2,8,32]{0,3,2,1:T(8,128)(2,1)S(1)}, u32[]{:S(2)}, u32[]{:S(2)}) collective-permute-start(bf16[256,2,8,32]{0,3,2,1:T(8,128)(2,1)S(1)} %get-tuple-element.346), channel_id=1, source_target_pairs={{0,28},{4,0},{8,4},{12,8},{16,12},{20,16},{24,20},{28,24},{1,29},{... | collective-permute-start | bytes 786440 | tf_op jit(solution)/shard_map/while/body/eval_jaxpr/ppermute | solution.py:40
  189.6 3.9 %collective-permute-done = bf16[256,2,8,32]{0,3,2,1:T(8,128)(2,1)S(1)} collective-permute-done((bf16[256,2,8,32]{0,3,2,1:T(8,128)(2,1)S(1)}, bf16[256,2,8,32]{0,3,2,1:T(8,128)(2,1)S(1)}, u32[]{:S(2)}, u32[]{:S(2)}) %collective-permute-start) | collective-permute-done | bytes 262176 | tf_op jit(solution)/shard_map/while/body/eval_jaxpr/ppermute | solution.py:40
  194.4 1.6 convolution_bitcast_fusion.6
  200.0 4.6 %collective-permute-start.6 = (bf16[256,2,8,8]{0,3,2,1:T(8,128)(2,1)S(1)}, bf16[256,2,8,8]{0,3,2,1:T(8,128)(2,1)S(1)}, u32[]{:S(2)}, u32[]{:S(2)}) collective-permute-start(bf16[256,2,8,8]{0,3,2,1:T(8,128)(2,1)S(1)} %get-tuple-element.252), channel_id=1, source_target_pairs={{0,16},{4,20},{8,24},{12,28},{16,0},{20,4},{24,8},{28,12},{1,17},{... | collective-permute-start | bytes 196616 | tf_op jit(solution)/shard_map/ppermute | solution.py:26
  204.5 2.3 %collective-permute-start.7 = (bf16[256,2,8,8]{0,3,2,1:T(8,128)(2,1)S(1)}, bf16[256,2,8,8]{0,3,2,1:T(8,128)(2,1)S(1)}, u32[]{:S(2)}, u32[]{:S(2)}) collective-permute-start(bf16[256,2,8,8]{0,3,2,1:T(8,128)(2,1)S(1)} %get-tuple-element.251), channel_id=1, source_target_pairs={{0,20},{4,24},{8,28},{12,0},{16,4},{20,8},{24,12},{28,16},{1,21},{... | collective-permute-start | bytes 196616 | tf_op jit(solution)/shard_map/ppermute | solution.py:26
  209.0 2.9 %collective-permute-done.5 = bf16[256,2,8,8]{0,3,2,1:T(8,128)(2,1)S(1)} collective-permute-done((bf16[256,2,8,8]{0,3,2,1:T(8,128)(2,1)S(1)}, bf16[256,2,8,8]{0,3,2,1:T(8,128)(2,1)S(1)}, u32[]{:S(2)}, u32[]{:S(2)}) %collective-permute-start.5) | collective-permute-done | bytes 65568 | tf_op jit(solution)/shard_map/ppermute | solution.py:26
  212.0 2.2 %collective-permute-done.8 = bf16[256,2,8,8]{0,3,2,1:T(8,128)(2,1)S(1)} collective-permute-done((bf16[256,2,8,8]{0,3,2,1:T(8,128)(2,1)S(1)}, bf16[256,2,8,8]{0,3,2,1:T(8,128)(2,1)S(1)}, u32[]{:S(2)}, u32[]{:S(2)}) %collective-permute-start.8) | collective-permute-done | bytes 65568 | tf_op jit(solution)/shard_map/ppermute | solution.py:26
  (96 shorter events, 29.9 us)
Async XLA Ops:
  0.0 99.4 %collective-permute-start.1 = (bf16[8,8,2,1024]{3,2,1,0:T(2,128)(2,1)}, bf16[8,8,2,1024]{3,2,1,0:T(2,128)(2,1)S(1)}, u32[]{:S(2)}, u32[]{:S(2)}) collective-permute-start(bf16[8,8,2,1024]{3,2,1,0:T(2,128)(2,1)} %param.4), channel_id=1, source_target_pairs={{0,1},{1,2},{2,3},{4,5},{5,6},{6,7},{8,9},{9,10},{10,11},{12,13},{... | collective-permute-start | bytes 786440 | tf_op jit(solution)/shard_map/ppermute | solution.py:34
  6.0 93.2 %collective-permute-start.2 = (bf16[8,7,2,1024]{3,2,1,0:T(2,128)(2,1)S(1)}, bf16[8,7,2,1024]{3,2,1,0:T(2,128)(2,1)S(1)}, u32[]{:S(2)}, u32[]{:S(2)}) collective-permute-start(bf16[8,7,2,1024]{3,2,1,0:T(2,128)(2,1)S(1)} %slice.151), channel_id=1, source_target_pairs={{0,2},{1,3},{4,6},{5,7},{8,10},{9,11},{12,14},{13,15},{16,18},{17,... | collective-permute-start | bytes 688136 | tf_op jit(solution)/shard_map/ppermute | solution.py:34
  85.0 14.2 %copy-start.3 = (f32[16,1024]{1,0:T(8,128)S(1)}, f32[16,1024]{1,0:T(8,128)}, u32[]{:S(2)}) copy-start(f32[16,1024]{1,0:T(8,128)} %param.5) | copy-start | bytes 196612
  85.0 14.9 %copy-start.2 = (bf16[8,8,2,1024]{3,2,1,0:T(2,128)(2,1)S(1)}, bf16[8,8,2,1024]{3,2,1,0:T(2,128)(2,1)}, u32[]{:S(2)}) copy-start(bf16[8,8,2,1024]{3,2,1,0:T(2,128)(2,1)} %param.4) | copy-start | bytes 786436
  123.4 8.8 %all-to-all-start = ((bf16[4,2,16384]{2,1,0:T(2,128)(2,1)}), bf16[4,2,16384]{2,1,0:T(2,128)(2,1)S(1)}, u32[]{:S(2)}, u32[]{:S(2)}) async-start(bf16[4,2,16384]{2,1,0:T(2,128)(2,1)} %reshape.208), calls=%async_computation | async-start | bytes 524288 | tf_op jit(solution)/shard_map/all_to_all | solution.py:104
  148.6 1.1 copy-start
  149.8 5.2 %collective-permute-start = (bf16[256,2,8,32]{0,3,2,1:T(8,128)(2,1)S(1)}, bf16[256,2,8,32]{0,3,2,1:T(8,128)(2,1)S(1)}, u32[]{:S(2)}, u32[]{:S(2)}) collective-permute-start(bf16[256,2,8,32]{0,3,2,1:T(8,128)(2,1)S(1)} %get-tuple-element.346), channel_id=1, source_target_pairs={{0,28},{4,0},{8,4},{12,8},{16,12},{20,16},{24,20},{28,24},{1,29},{... | collective-permute-start | bytes 786440 | tf_op jit(solution)/shard_map/while/body/eval_jaxpr/ppermute | solution.py:40
  160.2 7.6 %collective-permute-start = (bf16[256,2,8,32]{0,3,2,1:T(8,128)(2,1)S(1)}, bf16[256,2,8,32]{0,3,2,1:T(8,128)(2,1)S(1)}, u32[]{:S(2)}, u32[]{:S(2)}) collective-permute-start(bf16[256,2,8,32]{0,3,2,1:T(8,128)(2,1)S(1)} %get-tuple-element.346), channel_id=1, source_target_pairs={{0,28},{4,0},{8,4},{12,8},{16,12},{20,16},{24,20},{28,24},{1,29},{... | collective-permute-start | bytes 786440 | tf_op jit(solution)/shard_map/while/body/eval_jaxpr/ppermute | solution.py:40
  173.0 7.6 %collective-permute-start = (bf16[256,2,8,32]{0,3,2,1:T(8,128)(2,1)S(1)}, bf16[256,2,8,32]{0,3,2,1:T(8,128)(2,1)S(1)}, u32[]{:S(2)}, u32[]{:S(2)}) collective-permute-start(bf16[256,2,8,32]{0,3,2,1:T(8,128)(2,1)S(1)} %get-tuple-element.346), channel_id=1, source_target_pairs={{0,28},{4,0},{8,4},{12,8},{16,12},{20,16},{24,20},{28,24},{1,29},{... | collective-permute-start | bytes 786440 | tf_op jit(solution)/shard_map/while/body/eval_jaxpr/ppermute | solution.py:40
  185.8 7.6 %collective-permute-start = (bf16[256,2,8,32]{0,3,2,1:T(8,128)(2,1)S(1)}, bf16[256,2,8,32]{0,3,2,1:T(8,128)(2,1)S(1)}, u32[]{:S(2)}, u32[]{:S(2)}) collective-permute-start(bf16[256,2,8,32]{0,3,2,1:T(8,128)(2,1)S(1)} %get-tuple-element.346), channel_id=1, source_target_pairs={{0,28},{4,0},{8,4},{12,8},{16,12},{20,16},{24,20},{28,24},{1,29},{... | collective-permute-start | bytes 786440 | tf_op jit(solution)/shard_map/while/body/eval_jaxpr/ppermute | solution.py:40
  199.8 7.9 %collective-permute-start.3 = (bf16[256,2,8,8]{0,3,2,1:T(8,128)(2,1)S(1)}, bf16[256,2,8,8]{0,3,2,1:T(8,128)(2,1)S(1)}, u32[]{:S(2)}, u32[]{:S(2)}) collective-permute-start(bf16[256,2,8,8]{0,3,2,1:T(8,128)(2,1)S(1)} %get-tuple-element.255), channel_id=1, source_target_pairs={{0,4},{4,8},{8,12},{12,16},{16,20},{20,24},{24,28},{28,0},{1,5},{5... | collective-permute-start | bytes 196616 | tf_op jit(solution)/shard_map/ppermute | solution.py:26
  199.8 7.9 %collective-permute-start.4 = (bf16[256,2,8,8]{0,3,2,1:T(8,128)(2,1)S(1)}, bf16[256,2,8,8]{0,3,2,1:T(8,128)(2,1)S(1)}, u32[]{:S(2)}, u32[]{:S(2)}) collective-permute-start(bf16[256,2,8,8]{0,3,2,1:T(8,128)(2,1)S(1)} %get-tuple-element.254), channel_id=1, source_target_pairs={{0,8},{4,12},{8,16},{12,20},{16,24},{20,28},{24,0},{28,4},{1,9},{5... | collective-permute-start | bytes 196616 | tf_op jit(solution)/shard_map/ppermute | solution.py:26
  199.9 11.9 %collective-permute-start.5 = (bf16[256,2,8,8]{0,3,2,1:T(8,128)(2,1)S(1)}, bf16[256,2,8,8]{0,3,2,1:T(8,128)(2,1)S(1)}, u32[]{:S(2)}, u32[]{:S(2)}) collective-permute-start(bf16[256,2,8,8]{0,3,2,1:T(8,128)(2,1)S(1)} %get-tuple-element.253), channel_id=1, source_target_pairs={{0,12},{4,16},{8,20},{12,24},{16,28},{20,0},{24,4},{28,8},{1,13},{... | collective-permute-start | bytes 196616 | tf_op jit(solution)/shard_map/ppermute | solution.py:26
  200.0 12.0 %collective-permute-start.6 = (bf16[256,2,8,8]{0,3,2,1:T(8,128)(2,1)S(1)}, bf16[256,2,8,8]{0,3,2,1:T(8,128)(2,1)S(1)}, u32[]{:S(2)}, u32[]{:S(2)}) collective-permute-start(bf16[256,2,8,8]{0,3,2,1:T(8,128)(2,1)S(1)} %get-tuple-element.252), channel_id=1, source_target_pairs={{0,16},{4,20},{8,24},{12,28},{16,0},{20,4},{24,8},{28,12},{1,17},{... | collective-permute-start | bytes 196616 | tf_op jit(solution)/shard_map/ppermute | solution.py:26
  204.5 7.5 %collective-permute-start.7 = (bf16[256,2,8,8]{0,3,2,1:T(8,128)(2,1)S(1)}, bf16[256,2,8,8]{0,3,2,1:T(8,128)(2,1)S(1)}, u32[]{:S(2)}, u32[]{:S(2)}) collective-permute-start(bf16[256,2,8,8]{0,3,2,1:T(8,128)(2,1)S(1)} %get-tuple-element.251), channel_id=1, source_target_pairs={{0,20},{4,24},{8,28},{12,0},{16,4},{20,8},{24,12},{28,16},{1,21},{... | collective-permute-start | bytes 196616 | tf_op jit(solution)/shard_map/ppermute | solution.py:26
  207.7 6.5 %collective-permute-start.8 = (bf16[256,2,8,8]{0,3,2,1:T(8,128)(2,1)S(1)}, bf16[256,2,8,8]{0,3,2,1:T(8,128)(2,1)S(1)}, u32[]{:S(2)}, u32[]{:S(2)}) collective-permute-start(bf16[256,2,8,8]{0,3,2,1:T(8,128)(2,1)S(1)} %get-tuple-element.250), channel_id=1, source_target_pairs={{0,24},{4,28},{8,0},{12,4},{16,8},{20,12},{24,16},{28,20},{1,25},{... | collective-permute-start | bytes 196616 | tf_op jit(solution)/shard_map/ppermute | solution.py:26
  207.7 6.5 %collective-permute-start.9 = (bf16[256,2,8,8]{0,3,2,1:T(8,128)(2,1)S(1)}, bf16[256,2,8,8]{0,3,2,1:T(8,128)(2,1)S(1)}, u32[]{:S(2)}, u32[]{:S(2)}) collective-permute-start(bf16[256,2,8,8]{0,3,2,1:T(8,128)(2,1)S(1)} %get-tuple-element.249), channel_id=1, source_target_pairs={{0,28},{4,0},{8,4},{12,8},{16,12},{20,16},{24,20},{28,24},{1,29},{... | collective-permute-start | bytes 196616 | tf_op jit(solution)/shard_map/ppermute | solution.py:26
  214.2 1.2 copy-start.1
